TPU v7x, 32 devices: a whole 2x2x4 slice. The times are simulated.
32 devices in a mesh: gx: 16 (over z, y, core), gy: 2 (over x).
Axes of the slice: x: 2, y: 2, z: 4, core: 2. Of those that a mesh axis runs over, the one named last changes fastest.
Arguments:
- field: float32 [6, 16, 256, 256], P(None, None, 'gx', 'gy'), may hold values from -6 to 6
- driver: float32 [6, 16, 256, 256], P(None, None, 'gx', 'gy'), may hold values from -6 to 6
- east_wind: float32 [16, 256, 256], P(None, 'gx', 'gy'), may hold values from -0.4 to 0.4
- north_wind: float32 [16, 256, 256], P(None, 'gx', 'gy'), may hold values from -0.4 to 0.4
Outputs:
- advected: float32 [6, 16, 256, 256], P(None, None, 'gx', 'gy')
- coeffs: float32 [6, 16, 4096], replicated
All inputs are finite; a program needn't handle non-finite values.
Results may differ from a plain program's by a relative error of at most 0.000098.
Values sent between devices are 32-bit elements; how exact they have to be, the bound alone decides.
A program may use at most 128 MiB of HBM per device.

v0:
```python
import math

import jax
import jax.numpy as jnp
from jax import lax
from jax.sharding import PartitionSpec as P

MX = 64
MY = 64


def shifted(value, axis, steps):
    count = lax.axis_size(axis)
    first, last = (max(0, -steps), min(count, count - steps))
    return lax.ppermute(value, axis, [(source, source + steps) for source in range(first, last)])


def padded(x, sides, width):
    for axis, dim in sides:
        peers, length = (lax.axis_size(axis), x.shape[dim])
        up = [(i, (i + 1) % peers) for i in range(peers - 1)]
        down = [(j, i) for i, j in up]
        last = lax.slice_in_dim(x, length - width, length, axis=dim)
        first = lax.slice_in_dim(x, 0, width, axis=dim)
        before = lax.ppermute(last, axis, up)
        after = lax.ppermute(first, axis, down)
        x = jnp.concatenate([before, x, after], axis=dim)
    return x


def cosine_table(first, count, total, modes):
    indices = first + jnp.arange(count, dtype=jnp.int32)
    wavenum = jnp.arange(modes, dtype=jnp.int32)
    phases = (wavenum[None, :] * (2 * indices[:, None] + 1)).astype(jnp.float32)
    cosines = jnp.cos(phases * (math.pi / (2.0 * total)))
    weight = jnp.where(wavenum == 0, math.sqrt(1.0 / total), math.sqrt(2.0 / total)).astype(
        jnp.float32
    )
    return cosines * weight[None, :]


def upwind(tracer, winds):
    east = winds[0]
    north = winds[1]
    east_flux = (
        jnp.maximum(east[:, :-1, :], 0.0) * tracer[..., :-1, :]
        + jnp.minimum(east[:, :-1, :], 0.0) * tracer[..., 1:, :]
    )
    north_flux = (
        jnp.maximum(north[:, :, :-1], 0.0) * tracer[..., :, :-1]
        + jnp.minimum(north[:, :, :-1], 0.0) * tracer[..., :, 1:]
    )
    inner = tracer[..., 1:-1, 1:-1]
    inner = inner - (east_flux[..., 1:, 1:-1] - east_flux[..., :-1, 1:-1])
    return inner - (north_flux[..., 1:-1, 1:] - north_flux[..., 1:-1, :-1])


def shards(field, driver, east_wind, north_wind):
    high = lax.Precision.HIGHEST
    tracers, levels, strip_cols, band_rows = field.shape
    nx_total = strip_cols * lax.axis_size("gx")
    ny_total = band_rows * lax.axis_size("gy")
    x_first = lax.axis_index("gx") * strip_cols
    y_first = lax.axis_index("gy") * band_rows
    x_table = cosine_table(x_first, strip_cols, nx_total, MX)
    y_table = cosine_table(y_first, band_rows, ny_total, MY)
    departure = driver - field
    half_proj = jnp.einsum("tlxy,xm->tlmy", departure, x_table, precision=high)
    partial_modes = jnp.einsum("tlmy,yn->tlmn", half_proj, y_table, precision=high)
    partial_modes = partial_modes.reshape(tracers, levels, MX * MY)
    coeffs = lax.psum(partial_modes, ("gx", "gy"))
    modal = coeffs.reshape(tracers, levels, MX, MY)
    large_scale = jnp.einsum("tlmn,yn->tlmy", modal, y_table, precision=high)
    large_scale = jnp.einsum("tlmy,xm->tlxy", large_scale, x_table, precision=high)
    nudged = field + 0.5 * large_scale
    xpos = x_first + jnp.arange(strip_cols, dtype=jnp.int32)
    ypos = y_first + jnp.arange(band_rows, dtype=jnp.int32)
    east_face = jnp.where(xpos[None, :, None] == nx_total - 1, jnp.float32(0.0), east_wind)
    north_face = jnp.where(ypos[None, None, :] == ny_total - 1, jnp.float32(0.0), north_wind)
    east_below = shifted(east_face[:, -1:, :], "gx", 1)
    north_below = shifted(north_face[:, :, -1:], "gy", 1)
    east_ext = jnp.concatenate([east_below, east_face, jnp.zeros_like(east_below)], axis=1)
    east_ext = jnp.pad(east_ext, ((0, 0), (0, 0), (1, 1)))
    north_ext = jnp.concatenate([north_below, north_face, jnp.zeros_like(north_below)], axis=2)
    north_ext = jnp.pad(north_ext, ((0, 0), (1, 1), (0, 0)))
    wind_ext = jnp.stack([east_ext, north_ext])
    advected = nudged
    for sweep in range(2):
        field_ext = padded(advected, (("gx", 2), ("gy", 3)), 1)
        advected = upwind(field_ext, wind_ext)
    return (advected, coeffs)


def solution(mesh):
    placed = (
        P(None, None, "gx", "gy"),
        P(None, None, "gx", "gy"),
        P(None, "gx", "gy"),
        P(None, "gx", "gy"),
    )
    return jax.shard_map(
        shards,
        mesh=mesh,
        in_specs=placed,
        out_specs=(P(None, None, "gx", "gy"), P()),
        check_vma=False,
    )
```

profile of v0, /device:TPU:8, one launch (start us, length us, event | category | flops | bytes accessed | tf_op | source)
XLA Modules:
  0.0 223.3 jit_solution(13646085363777777054)
XLA Ops:
  7.2 0.0 all-reduce.4.cloned.1.call-start
  7.3 0.5 copy-done.19
  7.8 4.2 %fusion.12 = f32[64,6,16,128]{3,0,2,1:T(8,128)S(1)} fusion(f32[6,16,16,128]{3,2,1,0:T(8,128)} %param.5, f32[6,16,16,128]{3,2,1,0:T(8,128)} %param.4, f32[64]{0:T(128)S(1)} %compare_select_fusion, s32[16]{0:T(128)S(1)} %multiply_add_fusion.1), kind=kOutput, calls=%fused_computation.29 | convolution fusion | flops 151195648 | bytes 4718912 | tf_op jit(solution)/shard_map/tlxy,xm->tlmy/dot_general | solution.py:68
  12.0 2.7 %fusion = f32[6,16,64,64]{3,2,1,0:T(8,128)S(1)} fusion(f32[64,6,16,128]{3,0,2,1:T(8,128)S(1)} %fusion.12, f32[64]{0:T(128)S(1)} %compare_select_fusion, s32[128]{0:T(128)S(1)} %multiply_add_fusion), kind=kOutput, calls=%fused_computation | convolution fusion | flops 604012544 | bytes 4719360 | tf_op jit(solution)/shard_map/tlmy,yn->tlmn/dot_general | solution.py:69
  14.7 0.0 copy-start.15
  14.7 0.0 copy-start.16
  14.7 1.9 reshape.47
  16.6 0.0 all-reduce.4.cloned.1.call-update
  16.7 0.1 slice.119
  16.8 3.4 %collective-permute-start.5 = (f32[16,16,1]{2,1,0:T(8,128)S(1)}, f32[16,16,1]{2,1,0:T(8,128)S(1)}, u32[]{:S(2)}, u32[]{:S(2)}) collective-permute-start(f32[16,16,1]{2,1,0:T(8,128)S(1)} %slice.119), channel_id=1, source_target_pairs={{0,1},{2,3},{4,5},{6,7},{8,9},{10,11},{12,13},{14,15},{16,17},{18,... | collective-permute-start | bytes 3080 | tf_op jit(solution)/shard_map/ppermute | solution.py:15
  20.2 0.1 broadcast_select_fusion.1
  20.3 2.1 collective-permute-start
  22.5 0.1 pad.36.clone
  22.5 0.7 pad.47.clone
  23.2 0.1 maximum_maximum_fusion
  23.3 0.8 fusion.17
  24.1 125.8 %all-reduce.4.cloned.1.call-done = f32[6,16,4096]{2,1,0:T(8,128)} async-done(((f32[6,16,4096]{2,1,0:T(8,128)}), f32[6,16,4096]{2,1,0:T(8,128)}) %all-reduce.4.cloned.1.call-update) | async-done | bytes 1572880 | tf_op jit(solution)/shard_map/psum | solution.py:71
  149.9 2.4 %reshape.48 = f32[6,16,64,64]{3,2,1,0:T(8,128)S(1)} reshape(f32[6,16,4096]{2,1,0:T(8,128)} %all-reduce.4.cloned.1.call-done) | data formatting | bytes 3145728 | tf_op jit(solution)/shard_map/reshape | solution.py:72
  152.3 0.0 copy-start.8
  152.3 3.6 %fusion.18 = f32[6,16,64,128]{3,2,1,0:T(8,128)S(1)} fusion(f32[6,16,64,64]{3,2,1,0:T(8,128)S(1)} %reshape.48, f32[64]{0:T(128)} %copy-done.17, s32[128]{0:T(128)} %copy-done.21), kind=kOutput, calls=%fused_computation.41 | convolution fusion | flops 604012544 | bytes 4719360 | tf_op jit(solution)/shard_map/tlmn,yn->tlmy/dot_general | solution.py:73
  156.0 1.7 fusion.7
  157.7 0.1 fusion.44
  157.7 1.9 collective-permute-start.2
  159.7 2.4 %collective-permute-start.1 = (f32[6,16,1,128]{3,2,1,0:T(1,128)S(1)}, f32[6,16,1,128]{3,2,1,0:T(1,128)S(1)}, u32[]{:S(2)}, u32[]{:S(2)}) collective-permute-start(f32[6,16,1,128]{3,2,1,0:T(1,128)S(1)} %get-tuple-element.8), channel_id=1, source_target_pairs={{0,2},{2,4},{4,6},{6,8},{8,10},{10,12},{12,14},{14,16},{16,18},{18... | collective-permute-start | bytes 147464 | tf_op jit(solution)/shard_map/ppermute | solution.py:25
  162.1 0.8 maximum_maximum_fusion.1
  162.9 3.1 %collective-permute-done.1 = f32[6,16,1,128]{3,2,1,0:T(1,128)S(1)} collective-permute-done((f32[6,16,1,128]{3,2,1,0:T(1,128)S(1)}, f32[6,16,1,128]{3,2,1,0:T(1,128)S(1)}, u32[]{:S(2)}, u32[]{:S(2)}) %collective-permute-start.1) | collective-permute-done | bytes 49184 | tf_op jit(solution)/shard_map/ppermute | solution.py:25
  166.0 0.2 pad_maximum_fusion.2
  166.2 0.4 fusion.42
  166.6 0.0 copy-done.13
  166.6 1.3 copy.6
  167.9 3.3 %collective-permute-start.3 = (f32[6,16,18,1]{2,1,3,0:T(8,128)}, f32[6,16,18,1]{2,1,3,0:T(8,128)S(1)}, u32[]{:S(2)}, u32[]{:S(2)}) collective-permute-start(f32[6,16,18,1]{2,1,3,0:T(8,128)} %copy.6), channel_id=1, source_target_pairs={{0,1},{2,3},{4,5},{6,7},{8,9},{10,11},{12,13},{14,15},{16,17},{18,... | collective-permute-start | bytes 20744 | tf_op jit(solution)/shard_map/ppermute | solution.py:25
  171.2 0.7 copy.7
  171.9 1.3 collective-permute-start.4
  173.1 2.2 fusion.15
  175.3 0.7 copy.8
  176.0 1.9 collective-permute-done.4
  177.9 1.5 copy.9
  179.4 2.3 %pad_maximum_fusion = f32[6,16,18,130]{3,2,1,0:T(8,128)S(1)} fusion(f32[6,16,18,1]{3,2,1,0:T(8,128)S(1)} %copy.9, f32[6,16,1,128]{3,2,1,0:T(1,128)} %copy-done.11, f32[6,16,16,128]{3,2,1,0:T(8,128)S(1)} %fusion.7, f32[6,16,1,128]{3,2,1,0:T(1,128)} %copy-done.13, f32[6,16,18,1]{3,2,1,0:T(8,128)S(1)} %copy.8), kind=kLoop, calls=%fused_computation.8 | loop fusion | flops 898560 | bytes 1797120 | tf_op jit(solution)/shard_map/concatenate | solution.py:27
  181.8 0.0 copy-start.2
  181.8 0.4 fusion.3
  182.2 0.5 copy-done.2
  182.8 1.3 fusion.4
  184.0 0.7 fusion.10
  184.7 0.1 fusion.43
  184.8 1.9 collective-permute-start.7
  186.7 2.6 %collective-permute-start.6 = (f32[6,16,1,128]{3,2,1,0:T(1,128)S(1)}, f32[6,16,1,128]{3,2,1,0:T(1,128)S(1)}, u32[]{:S(2)}, u32[]{:S(2)}) collective-permute-start(f32[6,16,1,128]{3,2,1,0:T(1,128)S(1)} %get-tuple-element.6), channel_id=1, source_target_pairs={{0,2},{2,4},{4,6},{6,8},{8,10},{10,12},{12,14},{14,16},{16,18},{18... | collective-permute-start | bytes 147464 | tf_op jit(solution)/shard_map/ppermute | solution.py:25
  189.3 3.9 %collective-permute-done.6 = f32[6,16,1,128]{3,2,1,0:T(1,128)S(1)} collective-permute-done((f32[6,16,1,128]{3,2,1,0:T(1,128)S(1)}, f32[6,16,1,128]{3,2,1,0:T(1,128)S(1)}, u32[]{:S(2)}, u32[]{:S(2)}) %collective-permute-start.6) | collective-permute-done | bytes 49184 | tf_op jit(solution)/shard_map/ppermute | solution.py:25
  193.2 0.2 pad_maximum_fusion.3
  193.4 1.4 fusion.41
  194.8 1.9 copy.12
  196.7 3.2 %collective-permute-start.8 = (f32[6,16,18,1]{2,1,3,0:T(8,128)S(1)}, f32[6,16,18,1]{2,1,3,0:T(8,128)S(1)}, u32[]{:S(2)}, u32[]{:S(2)}) collective-permute-start(f32[6,16,18,1]{2,1,3,0:T(8,128)S(1)} %copy.12), channel_id=1, source_target_pairs={{0,1},{2,3},{4,5},{6,7},{8,9},{10,11},{12,13},{14,15},{16,17},{18,... | collective-permute-start | bytes 20744 | tf_op jit(solution)/shard_map/ppermute | solution.py:25
  200.0 0.7 copy.13
  200.7 1.3 collective-permute-start.9
  202.0 0.7 copy.14
  202.7 4.0 %collective-permute-done.9 = f32[6,16,18,1]{2,1,3,0:T(8,128)S(1)} collective-permute-done((f32[6,16,18,1]{2,1,3,0:T(8,128)S(1)}, f32[6,16,18,1]{2,1,3,0:T(8,128)S(1)}, u32[]{:S(2)}, u32[]{:S(2)}) %collective-permute-start.9) | collective-permute-done | bytes 6944 | tf_op jit(solution)/shard_map/ppermute | solution.py:26
  206.6 1.7 copy.15
  208.3 2.7 %pad_maximum_fusion.1 = f32[6,16,18,130]{3,2,1,0:T(8,128)S(1)} fusion(f32[6,16,18,1]{3,2,1,0:T(8,128)} %copy.15, f32[6,16,1,128]{3,2,1,0:T(1,128)S(1)} %collective-permute-done.7, f32[6,16,16,128]{3,2,1,0:T(8,128)S(1)} %fusion.10, f32[6,16,1,128]{3,2,1,0:T(1,128)S(1)} %collective-permute-done.6, f32[6,16,18,1]{3,2,1,0:T(8,128)S(1)} %copy.14), kind=kLoop, calls=%fused_computation.12 | loop fusion | flops 898560 | bytes 1797120 | tf_op jit(solution)/shard_map/concatenate | solution.py:27
  211.1 0.0 copy-start
  211.1 0.4 fusion.2
  211.6 0.8 copy-done
  212.4 0.1 copy-done.3
  212.4 1.3 fusion.5
  213.7 1.6 fusion.8
  215.3 1.1 copy.21
  (49 shorter events, 0.1 us)
Async XLA Ops:
  7.2 142.7 %all-reduce.4.cloned.1.call-start = ((), (), s32[]{:S(2)}) async-start(), calls=%async_computation | async-start | bytes 3145728 | tf_op jit(solution)/shard_map/psum | solution.py:71
  7.2 4.7 %copy-start.17 = (f32[64]{0:T(128)}, f32[64]{0:T(128)S(1)}, u32[]{:S(2)}) copy-start(f32[64]{0:T(128)S(1)} %compare_select_fusion) | copy-start | bytes 772
  7.2 0.5 copy-start.19
  7.8 4.2 %copy-start.21 = (s32[128]{0:T(128)}, s32[128]{0:T(128)S(1)}, u32[]{:S(2)}) copy-start(s32[128]{0:T(128)S(1)} %multiply_add_fusion) | copy-start | bytes 1540
  14.7 2.0 copy-start.15
  14.7 5.5 %copy-start.16 = (f32[16,16,128]{2,1,0:T(8,128)S(1)}, f32[16,16,128]{2,1,0:T(8,128)}, u32[]{:S(2)}) copy-start(f32[16,16,128]{2,1,0:T(8,128)} %param.6) | copy-start | bytes 393220
  16.8 6.4 %collective-permute-start.5 = (f32[16,16,1]{2,1,0:T(8,128)S(1)}, f32[16,16,1]{2,1,0:T(8,128)S(1)}, u32[]{:S(2)}, u32[]{:S(2)}) collective-permute-start(f32[16,16,1]{2,1,0:T(8,128)S(1)} %slice.119), channel_id=1, source_target_pairs={{0,1},{2,3},{4,5},{6,7},{8,9},{10,11},{12,13},{14,15},{16,17},{18,... | collective-permute-start | bytes 3080 | tf_op jit(solution)/shard_map/ppermute | solution.py:15
  20.3 2.9 %copy-start.9 = (f32[16,16,128]{2,1,0:T(8,128)}, f32[16,16,128]{2,1,0:T(8,128)S(1)}, u32[]{:S(2)}) copy-start(f32[16,16,128]{2,1,0:T(8,128)S(1)} %broadcast_select_fusion.1) | copy-start | bytes 393220
  20.3 141.7 %collective-permute-start = (f32[16,1,128]{2,1,0:T(1,128)S(1)}, f32[16,1,128]{2,1,0:T(1,128)S(1)}, u32[]{:S(2)}, u32[]{:S(2)}) collective-permute-start(f32[16,1,128]{2,1,0:T(1,128)S(1)} %slice.110), channel_id=1, source_target_pairs={{0,2},{2,4},{4,6},{6,8},{8,10},{10,12},{12,14},{14,16},{16,18},{18... | collective-permute-start | bytes 24584 | tf_op jit(solution)/shard_map/ppermute | solution.py:15
  152.3 3.6 %copy-start.8 = (f32[6,16,16,128]{3,2,1,0:T(8,128)S(1)}, f32[6,16,16,128]{3,2,1,0:T(8,128)}, u32[]{:S(2)}) copy-start(f32[6,16,16,128]{3,2,1,0:T(8,128)} %param.4) | copy-start | bytes 2359300
  152.3 3.6 %copy-start.18 = (f32[64]{0:T(128)S(1)}, f32[64]{0:T(128)}, u32[]{:S(2)}) copy-start(f32[64]{0:T(128)} %copy-done.17) | copy-start | bytes 772
  152.3 3.6 %copy-start.20 = (s32[16]{0:T(128)S(1)}, s32[16]{0:T(128)}, u32[]{:S(2)}) copy-start(s32[16]{0:T(128)} %copy-done.19) | copy-start | bytes 196
  155.9 6.1 %copy-start.10 = (f32[16,16,128]{2,1,0:T(8,128)S(1)}, f32[16,16,128]{2,1,0:T(8,128)}, u32[]{:S(2)}) copy-start(f32[16,16,128]{2,1,0:T(8,128)} %copy-done.9) | copy-start | bytes 393220
  156.0 6.1 %copy-start.22 = (f32[18]{0:T(128)S(1)}, f32[18]{0:T(128)}, u32[]{:S(2)}) copy-start(f32[18]{0:T(128)} %pad.47.clone) | copy-start | bytes 220
  157.7 5.1 %collective-permute-start.2 = (f32[6,16,1,128]{3,2,1,0:T(1,128)S(1)}, f32[6,16,1,128]{3,2,1,0:T(1,128)S(1)}, u32[]{:S(2)}, u32[]{:S(2)}) collective-permute-start(f32[6,16,1,128]{3,2,1,0:T(1,128)S(1)} %get-tuple-element.9), channel_id=1, source_target_pairs={{2,0},{4,2},{6,4},{8,6},{10,8},{12,10},{14,12},{16,14},{18,16},{20... | collective-permute-start | bytes 147464 | tf_op jit(solution)/shard_map/ppermute | solution.py:26
  159.7 6.3 %collective-permute-start.1 = (f32[6,16,1,128]{3,2,1,0:T(1,128)S(1)}, f32[6,16,1,128]{3,2,1,0:T(1,128)S(1)}, u32[]{:S(2)}, u32[]{:S(2)}) collective-permute-start(f32[6,16,1,128]{3,2,1,0:T(1,128)S(1)} %get-tuple-element.8), channel_id=1, source_target_pairs={{0,2},{2,4},{4,6},{6,8},{8,10},{10,12},{12,14},{14,16},{16,18},{18... | collective-permute-start | bytes 147464 | tf_op jit(solution)/shard_map/ppermute | solution.py:25
  162.9 3.7 %copy-start.11 = (f32[6,16,1,128]{3,2,1,0:T(1,128)}, f32[6,16,1,128]{3,2,1,0:T(1,128)S(1)}, u32[]{:S(2)}) copy-start(f32[6,16,1,128]{3,2,1,0:T(1,128)S(1)} %collective-permute-done.2) | copy-start | bytes 147460
  166.0 0.6 copy-start.13
  167.9 7.5 %collective-permute-start.3 = (f32[6,16,18,1]{2,1,3,0:T(8,128)}, f32[6,16,18,1]{2,1,3,0:T(8,128)S(1)}, u32[]{:S(2)}, u32[]{:S(2)}) collective-permute-start(f32[6,16,18,1]{2,1,3,0:T(8,128)} %copy.6), channel_id=1, source_target_pairs={{0,1},{2,3},{4,5},{6,7},{8,9},{10,11},{12,13},{14,15},{16,17},{18,... | collective-permute-start | bytes 20744 | tf_op jit(solution)/shard_map/ppermute | solution.py:25
  171.9 6.1 %collective-permute-start.4 = (f32[6,16,18,1]{2,1,3,0:T(8,128)S(1)}, f32[6,16,18,1]{2,1,3,0:T(8,128)}, u32[]{:S(2)}, u32[]{:S(2)}) collective-permute-start(f32[6,16,18,1]{2,1,3,0:T(8,128)S(1)} %copy.7), channel_id=1, source_target_pairs={{1,0},{3,2},{5,4},{7,6},{9,8},{11,10},{13,12},{15,14},{17,16},{19,... | collective-permute-start | bytes 20744 | tf_op jit(solution)/shard_map/ppermute | solution.py:26
  179.4 2.3 %copy-start.4 = (f32[16,17,130]{2,1,0:T(8,128)S(1)}, f32[16,17,130]{2,1,0:T(8,128)}, u32[]{:S(2)}) copy-start(f32[16,17,130]{2,1,0:T(8,128)} %get-tuple-element.12) | copy-start | bytes 424324
  179.4 2.3 %copy-start.6 = (f32[16,17,130]{2,1,0:T(8,128)S(1)}, f32[16,17,130]{2,1,0:T(8,128)}, u32[]{:S(2)}) copy-start(f32[16,17,130]{2,1,0:T(8,128)} %get-tuple-element.13) | copy-start | bytes 424324
  181.8 1.0 copy-start.2
  181.8 1.0 copy-start.12
  181.8 1.0 copy-start.14
  184.8 4.6 %collective-permute-start.7 = (f32[6,16,1,128]{3,2,1,0:T(1,128)S(1)}, f32[6,16,1,128]{3,2,1,0:T(1,128)S(1)}, u32[]{:S(2)}, u32[]{:S(2)}) collective-permute-start(f32[6,16,1,128]{3,2,1,0:T(1,128)S(1)} %get-tuple-element.7), channel_id=1, source_target_pairs={{2,0},{4,2},{6,4},{8,6},{10,8},{12,10},{14,12},{16,14},{18,16},{20... | collective-permute-start | bytes 147464 | tf_op jit(solution)/shard_map/ppermute | solution.py:26
  186.7 6.5 %collective-permute-start.6 = (f32[6,16,1,128]{3,2,1,0:T(1,128)S(1)}, f32[6,16,1,128]{3,2,1,0:T(1,128)S(1)}, u32[]{:S(2)}, u32[]{:S(2)}) collective-permute-start(f32[6,16,1,128]{3,2,1,0:T(1,128)S(1)} %get-tuple-element.6), channel_id=1, source_target_pairs={{0,2},{2,4},{4,6},{6,8},{8,10},{10,12},{12,14},{14,16},{16,18},{18... | collective-permute-start | bytes 147464 | tf_op jit(solution)/shard_map/ppermute | solution.py:25
  196.7 5.2 %collective-permute-start.8 = (f32[6,16,18,1]{2,1,3,0:T(8,128)S(1)}, f32[6,16,18,1]{2,1,3,0:T(8,128)S(1)}, u32[]{:S(2)}, u32[]{:S(2)}) collective-permute-start(f32[6,16,18,1]{2,1,3,0:T(8,128)S(1)} %copy.12), channel_id=1, source_target_pairs={{0,1},{2,3},{4,5},{6,7},{8,9},{10,11},{12,13},{14,15},{16,17},{18,... | collective-permute-start | bytes 20744 | tf_op jit(solution)/shard_map/ppermute | solution.py:25
  200.7 6.0 %collective-permute-start.9 = (f32[6,16,18,1]{2,1,3,0:T(8,128)S(1)}, f32[6,16,18,1]{2,1,3,0:T(8,128)S(1)}, u32[]{:S(2)}, u32[]{:S(2)}) collective-permute-start(f32[6,16,18,1]{2,1,3,0:T(8,128)S(1)} %copy.13), channel_id=1, source_target_pairs={{1,0},{3,2},{5,4},{7,6},{9,8},{11,10},{13,12},{15,14},{17,16},{19,... | collective-permute-start | bytes 20744 | tf_op jit(solution)/shard_map/ppermute | solution.py:26
  208.3 2.7 %copy-start.5 = (f32[16,17,130]{2,1,0:T(8,128)S(1)}, f32[16,17,130]{2,1,0:T(8,128)}, u32[]{:S(2)}) copy-start(f32[16,17,130]{2,1,0:T(8,128)} %get-tuple-element.12) | copy-start | bytes 424324
  208.3 2.8 %copy-start.7 = (f32[16,17,130]{2,1,0:T(8,128)S(1)}, f32[16,17,130]{2,1,0:T(8,128)}, u32[]{:S(2)}) copy-start(f32[16,17,130]{2,1,0:T(8,128)} %get-tuple-element.13) | copy-start | bytes 424324
  211.1 1.3 copy-start
  211.1 1.3 copy-start.3
  213.7 1.6 copy-start.1
Sparse Core Ops, SparseCore 0:
  16.8 133.0 all-reduce.3
where the time goes:
time: 224 us; the launch traced here: 223 us
  waiting for transfers between devices  139 us (62%)
  starting transfers between devices  23.5 us (10%)
  local copies, waits for them, and re-layouts  19.4 us (9%)
  other arithmetic  15 us (7%)
  between operations  14.6 us (7%)
  matrix products  12.1 us (5%)
    psum x1, waiting for transfers between devices, shards(): coeffs = lax.psum(partial_modes, ('gx', 'gy'))  126 us
    ppermute x4, starting transfers between devices, padded(): before = lax.ppermute(last, axis, up)  11.6 us
    ppermute x4, waiting for transfers between devices, padded(): before = lax.ppermute(last, axis, up)  6.99 us
    ppermute x4, starting transfers between devices, padded(): after = lax.ppermute(first, axis, down)  6.4 us
    ppermute x4, waiting for transfers between devices, padded(): after = lax.ppermute(first, axis, down)  5.89 us
    ppermute x2, starting transfers between devices, shifted(): lax.ppermute(value, axis, [(source, source + steps) for source in range(f...  5.5 us
    concatenate x4, other arithmetic, padded(): x = jnp.concatenate([before, x, after], axis=dim)  5.4 us
  transfers between devices with their start and end apart: 11, of which 5 were waited for; matrix products, arithmetic and copies ran while one was open for 7% of the time, Pallas kernels for 0%

commit v1 on v0

--- a/solution.py
+++ b/solution.py
@@ -2,11 +2,16 @@
 
 import jax
 import jax.numpy as jnp
+import ml_dtypes
+import numpy as np
 from jax import lax
+from jax.experimental import pallas as pl
+from jax.experimental.pallas import tpu as pltpu
 from jax.sharding import PartitionSpec as P
 
 MX = 64
 MY = 64
+MESH = pl.DeviceIdType.MESH
 
 
 def shifted(value, axis, steps):
@@ -91,6 +96,433 @@
     return (advected, coeffs)
 
 
+def split(value):
+    high = value.astype(jnp.bfloat16)
+    return high, (value - high.astype(jnp.float32)).astype(jnp.bfloat16)
+
+
+def split_table(table):
+    table = np.asarray(table, np.float32)
+    high = table.astype(ml_dtypes.bfloat16)
+    low = (table - high.astype(np.float32)).astype(ml_dtypes.bfloat16)
+    return high, low
+
+
+def table64(total, modes):
+    index = np.arange(total)[:, None]
+    wave = np.arange(modes)[None, :]
+    weight = np.where(wave == 0, math.sqrt(1.0 / total), math.sqrt(2.0 / total))
+    turns = (wave * (2 * index + 1)) % (4 * total)
+    return np.cos(turns * (math.pi / (2.0 * total))) * weight
+
+
+def dot(a, b):
+    return jnp.dot(a, b, preferred_element_type=jnp.float32)
+
+
+def tables(gxn, gyn, strip, band):
+    bx = table64(gxn * strip, MX)
+    by = table64(gyn * band, MY)
+    half = strip // 2
+    forward_y = np.zeros((gyn, 2 * band, 2 * MY))
+    for g in range(gyn):
+        own = by[g * band : (g + 1) * band]
+        forward_y[g, :band, :MY] = own
+        forward_y[g, band:, MY:] = own
+    wy = np.stack(split_table(forward_y), axis=1)
+    bx4 = bx.reshape(gxn, 2, half, MX // 2, 2)
+    forward_x = np.broadcast_to(
+        bx4.transpose(1, 4, 3, 0, 2)[:, :, :, :, None, :], (2, 2, MX // 2, gxn, gyn, half)
+    )
+    wx = np.stack(split_table(forward_x.reshape(2 * MX, gxn * gyn * half)))
+    inverse_x = np.zeros((gxn, 2, strip + 8, MX // 2))
+    for g in range(gxn):
+        for row in range(strip + 8):
+            if row < strip + 2:
+                x = g * strip + row
+            elif row >= strip + 6:
+                x = g * strip + row - strip - 8
+            else:
+                continue
+            if 0 <= x < gxn * strip:
+                inverse_x[g, :, row] = bx[x].reshape(MX // 2, 2).T
+    high, low = split_table(inverse_x.reshape(gxn, 2 * (strip + 8), MX // 2))
+    xb = np.concatenate([high, high, low], axis=2)
+    inverse_y = np.zeros((gyn, 2 * MY, gyn * band))
+    for g in range(gyn):
+        rolled = 0.5 * np.roll(by, -g * band, axis=0).T
+        inverse_y[g, :MY] = rolled
+        inverse_y[g, MY:] = rolled
+    wi = np.stack(split_table(inverse_y), axis=1)
+    return wy, wx, xb, wi
+
+
+def gather_kernel(
+    field, driver, east, north, wy, wx, coef, halo, ytile,
+    part, recv, edge, ysend, wind,
+    a2a_s, a2a_r, halo_s, halo_r, y_s, y_r, z_s, z_r, p2_s, p2_r, p3_s, p3_r, core_s, core_r,
+):
+    gx = lax.axis_index("gx")
+    gy = lax.axis_index("gy")
+    gxn, gyn = lax.axis_size("gx"), lax.axis_size("gy")
+    count = gxn * gyn
+    me = gx * gyn + gy
+    fields, strip, band = field.shape
+    levels = east.shape[0]
+    own = fields // count
+
+    barrier = pltpu.get_barrier_semaphore()
+
+    def greet(rel, carry):
+        d = (me + rel) % count
+        pl.semaphore_signal(
+            barrier, inc=1, device_id=(d // gyn, d % gyn), device_id_type=MESH
+        )
+        return carry
+
+    lax.fori_loop(1, count, greet, 0)
+
+    wh, wl = wy[gy, 0], wy[gy, 1]
+    chunk = 4 * own
+    for c in range(fields // chunk):
+        rows = pl.ds(c * chunk, chunk)
+        departure = driver[rows] - field[rows]
+        lhs = jnp.concatenate([departure[:, : strip // 2], departure[:, strip // 2 :]], axis=2)
+        high, low = split(lhs.reshape(chunk * strip // 2, 2 * band))
+        got = dot(high, wh) + (dot(low, wh) + dot(high, wl))
+        part[pl.ds(c * 4, 4)] = got.reshape(4, own, strip // 2, 2 * MY)
+    pl.semaphore_wait(barrier, count - 1)
+
+    def exchange(d, s):
+        return pltpu.make_async_remote_copy(
+            src_ref=part.at[d], dst_ref=recv.at[s], send_sem=a2a_s.at[d], recv_sem=a2a_r.at[s],
+            device_id=(d // gyn, d % gyn), device_id_type=MESH,
+        )
+
+    def send(rel, carry):
+        exchange((me + rel) % count, me).start()
+        return carry
+
+    lax.fori_loop(1, count, send, 0)
+    recv[me] = part[me]
+
+    row = lax.broadcasted_iota(jnp.int32, (levels, strip, band), 1) + gx * strip
+    wind[pl.ds(0, levels)] = jnp.where(row == gxn * strip - 1, 0.0, east[...])
+    col = lax.broadcasted_iota(jnp.int32, (levels, strip, band), 2) + gy * band
+    wind[pl.ds(levels, levels)] = jnp.where(col == gyn * band - 1, 0.0, north[...])
+
+    for side in range(2):
+        for k in range(2):
+            r = (strip - 2 if side == 0 else 0) + k
+            edge[side, k, pl.ds(0, fields)] = field[:, r, :]
+            edge[side, k, pl.ds(fields, 2 * levels)] = wind[:, r, :]
+
+    def halo_copy(side, dy):
+        peer = gx + 1 if side == 0 else gx - 1
+        return pltpu.make_async_remote_copy(
+            src_ref=edge.at[side], dst_ref=halo.at[side, dy],
+            send_sem=halo_s.at[side, dy], recv_sem=halo_r.at[side, dy],
+            device_id=(peer, (gy + dy) % gyn), device_id_type=MESH,
+        )
+
+    for dy in range(2):
+
+        @pl.when(gx < gxn - 1)
+        def _():
+            halo_copy(0, dy).start()
+
+        @pl.when(gx > 0)
+        def _():
+            halo_copy(1, dy).start()
+
+        @pl.when(gx == 0)
+        def _():
+            halo[0, dy] = jnp.zeros(halo.shape[2:], jnp.float32)
+
+        @pl.when(gx == gxn - 1)
+        def _():
+            halo[1, dy] = jnp.zeros(halo.shape[2:], jnp.float32)
+
+    for b in range((fields + 2 * levels) // 8):
+        if b * 8 < fields:
+            block = field[pl.ds(b * 8, 8)]
+        else:
+            block = wind[pl.ds(b * 8 - fields, 8)]
+        turned = block.reshape(8 * strip, band).T
+        ysend[b] = jnp.where(gy == 0, turned[band - 8 :], turned[:8])
+    ycopy = pltpu.make_async_remote_copy(
+        src_ref=ysend, dst_ref=ytile, send_sem=y_s, recv_sem=y_r,
+        device_id=(gx, 1 - gy), device_id_type=MESH,
+    )
+    ycopy.start()
+
+    def receive(rel, carry):
+        exchange((me + rel) % count, (me + rel) % count).wait_recv()
+        return carry
+
+    lax.fori_loop(1, count, receive, 0)
+    rhs = jnp.concatenate(
+        [recv[:, j].reshape(count * strip // 2, 2 * MY) for j in range(own)], axis=1
+    )
+    high, low = split(rhs)
+    modes = dot(wx[0], high) + (dot(wx[0], low) + dot(wx[1], high))
+    z, y, c, x = gx // 4, (gx // 2) % 2, gx % 2, gy
+    hm = MX // 2
+    lane = lax.broadcasted_iota(jnp.int32, (hm, 2 * MY), 1)
+    for j in range(own):
+        q = modes[:, j * 2 * MY : (j + 1) * 2 * MY]
+        even = q[:hm] + pltpu.roll(q[2 * hm : 3 * hm], MY, 1)
+        odd = pltpu.roll(q[hm : 2 * hm], MY, 1) + q[3 * hm :]
+        coef[z, y, c, x, pl.ds(j * hm, hm)] = jnp.where(lane < MY, even, odd)
+
+    part_rows = own * hm // 2
+    first, second = pl.ds(0, part_rows), pl.ds(part_rows, part_rows)
+    zs = [(z + k) % 4 for k in range(4)]
+
+    def z_copy(k, slot):
+        there = coef.at[slot, y, c, x]
+        return pltpu.make_async_remote_copy(
+            src_ref=there, dst_ref=there, send_sem=z_s.at[k], recv_sem=z_r.at[slot],
+            device_id=(zs[k] * 4 + y * 2 + c, gy), device_id_type=MESH,
+        )
+
+    def to_x(ref, s, r):
+        return pltpu.make_async_remote_copy(
+            src_ref=ref, dst_ref=ref, send_sem=s, recv_sem=r,
+            device_id=(gx, 1 - gy), device_id_type=MESH,
+        )
+
+    def to_y(ref, s, r):
+        return pltpu.make_async_remote_copy(
+            src_ref=ref, dst_ref=ref, send_sem=s, recv_sem=r,
+            device_id=(z * 4 + (1 - y) * 2 + c, gy), device_id_type=MESH,
+        )
+
+    def to_core(ref, s, r):
+        return pltpu.make_async_remote_copy(
+            src_ref=ref, dst_ref=ref, send_sem=s, recv_sem=r,
+            device_id=(z * 4 + y * 2 + 1 - c, gy), device_id_type=MESH,
+        )
+
+    def second_a(k, xx):
+        return to_x(coef.at[zs[k], y, c, xx, first], p2_s.at[0, k], p2_r.at[0, zs[k]])
+
+    def second_b(k, yy):
+        return to_y(coef.at[zs[k], yy, c, x, second], p2_s.at[1, k], p2_r.at[1, zs[k]])
+
+    def third_a(k, yy):
+        return to_y(coef.at[zs[k], yy, c, :, first], p3_s.at[0, k], p3_r.at[0, zs[k]])
+
+    def third_b(k, xx):
+        return to_x(coef.at[zs[k], :, c, xx, second], p3_s.at[1, k], p3_r.at[1, zs[k]])
+
+    def core_copy(k, cc):
+        return to_core(coef.at[zs[k], :, cc], core_s.at[k], core_r.at[zs[k]])
+
+    for k in range(1, 4):
+        z_copy(k, z).start()
+    for k in range(4):
+        if k:
+            z_copy(k, zs[k]).wait_recv()
+        second_a(k, x).start()
+        second_b(k, y).start()
+    for k in range(4):
+        second_a(k, 1 - x).wait_recv()
+        second_b(k, 1 - y).wait_recv()
+        third_a(k, y).start()
+        third_b(k, x).start()
+    for k in range(4):
+        third_a(k, 1 - y).wait_recv()
+        third_b(k, 1 - x).wait_recv()
+        core_copy(k, c).start()
+    for k in range(4):
+        core_copy(k, 1 - c).wait_recv()
+
+    for k in range(1, 4):
+        z_copy(k, z).wait_send()
+    for k in range(4):
+        second_a(k, x).wait_send()
+        second_b(k, y).wait_send()
+        third_a(k, y).wait_send()
+        third_b(k, x).wait_send()
+        core_copy(k, c).wait_send()
+
+    def drain(rel, carry):
+        exchange((me + rel) % count, me).wait_send()
+        return carry
+
+    lax.fori_loop(1, count, drain, 0)
+    ycopy.wait()
+    for dy in range(2):
+
+        @pl.when(gx < gxn - 1)
+        def _():
+            halo_copy(0, dy).wait_send()
+            halo_copy(1, dy).wait_recv()
+
+        @pl.when(gx > 0)
+        def _():
+            halo_copy(1, dy).wait_send()
+            halo_copy(0, dy).wait_recv()
+
+
+def advect_kernel(
+    field, east, north, coef, halo, ytile, xb, wi, out, coef_out, side, other, large
+):
+    gx = lax.axis_index("gx")
+    gy = lax.axis_index("gy")
+    gxn, gyn = lax.axis_size("gx"), lax.axis_size("gy")
+    fields, strip, band = field.shape
+    levels = east.shape[0]
+    tracers = fields // levels
+    ext = strip + 8
+    hm = MX // 2
+    total = fields + 2 * levels
+    for j in range(hm):
+        coef_out[:, pl.ds(j * 2 * MY, 2 * MY)] = coef[pl.ds(j, fields, stride=hm), :]
+    side[...] = jnp.zeros(side.shape, jnp.float32)
+    for d in range(2):
+        for k in range(2):
+            side[d, pl.ds(k, total, stride=8), :] = halo[1, d, k]
+            side[d, pl.ds(6 + k, total, stride=8), :] = halo[0, d, k]
+    gap = jnp.zeros((band - 16, 8 * strip), jnp.float32)
+    for b in range(total // 8):
+        tile = ytile[b]
+        spread = jnp.concatenate(
+            [jnp.where(gy == 0, tile, 0.0), gap, jnp.where(gy == 1, tile, 0.0)], axis=0
+        )
+        other[pl.ds(b * 8, 8)] = spread.T.reshape(8, strip, band)
+
+    table = xb[gx]
+    wh, wl = wi[gy, 0], wi[gy, 1]
+    lane = lax.broadcasted_iota(jnp.int32, (ext, 2 * MY), 1)
+    group = 4
+
+    def inverse(g, carry):
+        stack = []
+        for h in range(group // 2):
+            f = g * group + 2 * h
+            two = jnp.concatenate(
+                [
+                    coef[pl.ds(pl.multiple_of(f * hm, hm), hm), :],
+                    coef[pl.ds(pl.multiple_of(f * hm + hm, hm), hm), :],
+                ],
+                axis=1,
+            )
+            high, low = split(two)
+            mixed = dot(table, jnp.concatenate([high, low, high], axis=0))
+            for i in range(2):
+                one = mixed[:, i * 2 * MY : (i + 1) * 2 * MY]
+                stack.append(jnp.where(lane < MY, one[:ext], one[ext:]))
+        high, low = split(jnp.concatenate(stack, axis=0))
+        got = dot(high, wh) + (dot(low, wh) + dot(high, wl))
+        large[pl.ds(g * group, group)] = got.reshape(group, ext, gyn * band)
+        return carry
+
+    lax.fori_loop(0, fields // group, inverse, 0, unroll=2)
+
+    xpos = lax.broadcasted_iota(jnp.int32, (strip, band), 0) + gx * strip
+    ypos = lax.broadcasted_iota(jnp.int32, (strip, band), 1) + gy * band
+
+    def extend(own, f):
+        rows = pl.ds(pl.multiple_of(f * 8, 8), 8)
+        edge = jnp.concatenate([side[0, rows, :], side[1, rows, :]], axis=1)
+        return jnp.concatenate([jnp.concatenate([own, other[f]], axis=1), edge], axis=0)
+
+    def level(lev, carry):
+        east_own = jnp.where(xpos == gxn * strip - 1, 0.0, east[lev])
+        north_own = jnp.where(ypos == gyn * band - 1, 0.0, north[lev])
+        u = extend(east_own, fields + lev)
+        v = extend(north_own, fields + levels + lev)
+        up, un = jnp.maximum(u, 0.0), jnp.minimum(u, 0.0)
+        vp, vn = jnp.maximum(v, 0.0), jnp.minimum(v, 0.0)
+
+        def tracer(t, inner):
+            f = t * levels + lev
+            q = extend(field[f], f) + large[f]
+            for _ in range(2):
+                flux = up * q + un * pltpu.roll(q, ext - 1, 0)
+                cross = vp * q + vn * pltpu.roll(q, gyn * band - 1, 1)
+                q = q - (flux - pltpu.roll(flux, 1, 0))
+                q = q - (cross - pltpu.roll(cross, 1, 1))
+            out[f] = q[:strip, :band]
+            return inner
+
+        lax.fori_loop(0, tracers, tracer, 0, unroll=2)
+        return carry
+
+    lax.fori_loop(0, levels, level, 0)
+
+
+def fused(field, driver, east, north):
+    tracers, levels, strip, band = field.shape
+    gxn, gyn = lax.axis_size("gx"), lax.axis_size("gy")
+    count = gxn * gyn
+    fields = tracers * levels
+    own = fields // count
+    total = fields + 2 * levels
+    wy, wx, xb, wi = tables(gxn, gyn, strip, band)
+    flat = field.reshape(fields, strip, band)
+    dma = pltpu.SemaphoreType.DMA
+    vmem = pl.BlockSpec(memory_space=pltpu.VMEM)
+    f32 = jnp.float32
+    coef, halo, ytile = pl.pallas_call(
+        gather_kernel,
+        out_shape=(
+            jax.ShapeDtypeStruct((4, 2, 2, 2, own * MX // 2, 2 * MY), f32),
+            jax.ShapeDtypeStruct((2, 2, 2, total, band), f32),
+            jax.ShapeDtypeStruct((total // 8, 8, 8 * strip), f32),
+        ),
+        in_specs=[vmem] * 6,
+        out_specs=(vmem, vmem, vmem),
+        scratch_shapes=[
+            pltpu.VMEM((count, own, strip // 2, 2 * MY), f32),
+            pltpu.VMEM((count, own, strip // 2, 2 * MY), f32),
+            pltpu.VMEM((2, 2, total, band), f32),
+            pltpu.VMEM((total // 8, 8, 8 * strip), f32),
+            pltpu.VMEM((2 * levels, strip, band), f32),
+            dma((count,)), dma((count,)), dma((2, 2)), dma((2, 2)), dma, dma,
+            dma((4,)), dma((4,)), dma((2, 4)), dma((2, 4)), dma((2, 4)), dma((2, 4)),
+            dma((4,)), dma((4,)),
+        ],
+        compiler_params=pltpu.CompilerParams(
+            collective_id=0, has_side_effects=True, vmem_limit_bytes=40 << 20
+        ),
+        name="spectral_gather",
+    )(flat, driver.reshape(fields, strip, band), east, north, jnp.asarray(wy), jnp.asarray(wx))
+    advected, coeffs = pl.pallas_call(
+        advect_kernel,
+        out_shape=(
+            jax.ShapeDtypeStruct((fields, strip, band), f32),
+            jax.ShapeDtypeStruct((fields, MX * MY), f32),
+        ),
+        in_specs=[vmem] * 8,
+        out_specs=(vmem, vmem),
+        scratch_shapes=[
+            pltpu.VMEM((gyn, total * 8, band), f32),
+            pltpu.VMEM((total, strip, band), f32),
+            pltpu.VMEM((fields, strip + 8, gyn * band), f32),
+        ],
+        compiler_params=pltpu.CompilerParams(vmem_limit_bytes=40 << 20),
+        name="advect",
+    )(
+        flat, east, north, coef.reshape(fields * MX // 2, 2 * MY), halo, ytile,
+        jnp.asarray(xb), jnp.asarray(wi),
+    )
+    return (
+        advected.reshape(tracers, levels, strip, band),
+        coeffs.reshape(tracers, levels, MX * MY),
+    )
+
+
+def body(field, driver, east, north):
+    tracers, levels, strip, band = field.shape
+    sizes = (lax.axis_size("gx"), lax.axis_size("gy"))
+    if sizes == (16, 2) and (tracers * levels, levels, strip, band) == (96, 16, 16, 128):
+        return fused(field, driver, east, north)
+    return shards(field, driver, east, north)
+
+
 def solution(mesh):
     placed = (
         P(None, None, "gx", "gy"),
@@ -99,7 +531,7 @@
         P(None, "gx", "gy"),
     )
     return jax.shard_map(
-        shards,
+        body,
         mesh=mesh,
         in_specs=placed,
         out_specs=(P(None, None, "gx", "gy"), P()),

time: 224 us -> 61.6 us (0.28)
  the two profiles are of different devices: /device:TPU:8 before, /device:TPU:0 now
where the time goes in v1:
time: 61.6 us; the launch traced here: 61.2 us
  Pallas kernels  54.6 us (89%)
  local copies, waits for them, and re-layouts  5.93 us (10%)
  between operations  0.67 us (1%)
    pallas_call x1, Pallas kernels, fused(): pl.pallas_call(gather_kernel, out_shape=(jax.ShapeDtypeStruct((4, 2, 2, 2...  32.7 us
    pallas_call x1, Pallas kernels, fused(): pl.pallas_call(advect_kernel, out_shape=(jax.ShapeDtypeStruct((fields, st...  21.9 us
    unnamed x16, local copies, waits for them, and re-layouts  5.93 us

profile of v1, /device:TPU:0, one launch (start us, length us, event | category | flops | bytes accessed | tf_op | source)
XLA Modules:
  0.0 61.2 jit_solution(3241246532735266104)
XLA Ops:
  0.6 0.0 copy-start
  0.6 1.1 %copy-done = f32[6,16,16,128]{3,2,1,0:T(8,128)S(1)} copy-done((f32[6,16,16,128]{3,2,1,0:T(8,128)S(1)}, f32[6,16,16,128]{3,2,1,0:T(8,128)}, u32[]{:S(2)}) %copy-start) | copy-done | bytes 786456
  1.8 0.0 copy-start.1
  1.8 1.1 %copy-done.1 = f32[6,16,16,128]{3,2,1,0:T(8,128)S(1)} copy-done((f32[6,16,16,128]{3,2,1,0:T(8,128)S(1)}, f32[6,16,16,128]{3,2,1,0:T(8,128)}, u32[]{:S(2)}) %copy-start.1) | copy-done | bytes 786456
  2.9 0.0 copy-start.2
  2.9 0.9 %copy-done.2 = f32[16,16,128]{2,1,0:T(8,128)S(1)} copy-done((f32[16,16,128]{2,1,0:T(8,128)S(1)}, f32[16,16,128]{2,1,0:T(8,128)}, u32[]{:S(2)}) %copy-start.2) | copy-done | bytes 131096
  3.8 0.0 copy-start.3
  3.8 0.9 %copy-done.3 = f32[16,16,128]{2,1,0:T(8,128)S(1)} copy-done((f32[16,16,128]{2,1,0:T(8,128)S(1)}, f32[16,16,128]{2,1,0:T(8,128)}, u32[]{:S(2)}) %copy-start.3) | copy-done | bytes 131096
  4.7 0.0 copy-start.5
  4.7 0.9 %copy-done.5 = bf16[2,2,256,128]{3,2,1,0:T(8,128)(2,1)S(1)} copy-done((bf16[2,2,256,128]{3,2,1,0:T(8,128)(2,1)S(1)}, bf16[2,2,256,128]{3,2,1,0:T(8,128)(2,1)}, u32[]{:S(2)}) %copy-start.5) | copy-done | bytes 262168
  5.7 0.0 copy-start.7
  5.7 0.9 %copy-done.7 = bf16[2,128,256]{2,1,0:T(8,128)(2,1)S(1)} copy-done((bf16[2,128,256]{2,1,0:T(8,128)(2,1)S(1)}, bf16[2,128,256]{2,1,0:T(8,128)(2,1)}, u32[]{:S(2)}) %copy-start.7) | copy-done | bytes 131096
  6.6 0.0 copy-start.4
  6.6 0.0 copy-start.6
  6.6 32.7 %spectral_gather.1 = (f32[4,2,2,2,96,128]{5,4,3,2,1,0:T(8,128)S(1)}, f32[2,2,2,128,128]{4,3,2,1,0:T(8,128)S(1)}, f32[16,8,128]{2,1,0:T(8,128)S(1)}) custom-call(f32[96,16,128]{2,1,0:T(8,128)S(1)} %bitcast.5, f32[96,16,128]{2,1,0:T(8,128)S(1)} %bitcast.8, f32[16,16,128]{2,1,0:T(8,128)S(1)} %copy-done.2, f32[16,16,128]{2,1,0:T(8,128)S(1)} %copy-done.3, ...), custom_call_target="tpu_custom_call" | custom-call | tf_op jit(solution)/shard_map/spectral_gather/pallas_call | solution.py:469
  39.3 0.0 copy-done.4
  39.3 0.0 copy-done.6
  39.3 21.9 %advect.1 = (f32[96,16,128]{2,1,0:T(8,128)}, f32[96,4096]{1,0:T(8,128)}) custom-call(f32[96,16,128]{2,1,0:T(8,128)S(1)} %bitcast.6, f32[16,16,128]{2,1,0:T(8,128)S(1)} %copy-done.2, f32[16,16,128]{2,1,0:T(8,128)S(1)} %copy-done.3, f32[3072,128]{1,0:T(8,128)S(1)} %bitcast.7, f32[2,2,2,128,128]{4,3,2,1,0:T(8,128)S(1)} %get-tuple-element.8.halo, ...), custom_call_target="tpu_custom_call" | custom-call | tf_op jit(solution)/shard_map/advect/pallas_call | solution.py:493
Async XLA Ops:
  0.6 1.1 %copy-start = (f32[6,16,16,128]{3,2,1,0:T(8,128)S(1)}, f32[6,16,16,128]{3,2,1,0:T(8,128)}, u32[]{:S(2)}) copy-start(f32[6,16,16,128]{3,2,1,0:T(8,128)} %param.8) | copy-start | bytes 2359300
  1.8 1.1 %copy-start.1 = (f32[6,16,16,128]{3,2,1,0:T(8,128)S(1)}, f32[6,16,16,128]{3,2,1,0:T(8,128)}, u32[]{:S(2)}) copy-start(f32[6,16,16,128]{3,2,1,0:T(8,128)} %param.9) | copy-start | bytes 2359300
  2.9 0.9 %copy-start.2 = (f32[16,16,128]{2,1,0:T(8,128)S(1)}, f32[16,16,128]{2,1,0:T(8,128)}, u32[]{:S(2)}) copy-start(f32[16,16,128]{2,1,0:T(8,128)} %east.3) | copy-start | bytes 393220
  3.8 0.9 %copy-start.3 = (f32[16,16,128]{2,1,0:T(8,128)S(1)}, f32[16,16,128]{2,1,0:T(8,128)}, u32[]{:S(2)}) copy-start(f32[16,16,128]{2,1,0:T(8,128)} %north.3) | copy-start | bytes 393220
  4.7 0.9 %copy-start.5 = (bf16[2,2,256,128]{3,2,1,0:T(8,128)(2,1)S(1)}, bf16[2,2,256,128]{3,2,1,0:T(8,128)(2,1)}, u32[]{:S(2)}) copy-start(bf16[2,2,256,128]{3,2,1,0:T(8,128)(2,1)} %constant.8.clone.wy) | copy-start | bytes 786436
  5.7 0.9 %copy-start.7 = (bf16[2,128,256]{2,1,0:T(8,128)(2,1)S(1)}, bf16[2,128,256]{2,1,0:T(8,128)(2,1)}, u32[]{:S(2)}) copy-start(bf16[2,128,256]{2,1,0:T(8,128)(2,1)} %constant.9.clone.wx) | copy-start | bytes 393220
  6.6 32.7 %copy-start.4 = (bf16[2,2,128,256]{3,2,1,0:T(8,128)(2,1)S(1)}, bf16[2,2,128,256]{3,2,1,0:T(8,128)(2,1)}, u32[]{:S(2)}) copy-start(bf16[2,2,128,256]{3,2,1,0:T(8,128)(2,1)} %constant.11.clone.wi) | copy-start | bytes 786436
  6.6 32.7 %copy-start.6 = (bf16[16,48,96]{2,1,0:T(8,128)(2,1)S(1)}, bf16[16,48,96]{2,1,0:T(8,128)(2,1)}, u32[]{:S(2)}) copy-start(bf16[16,48,96]{2,1,0:T(8,128)(2,1)} %constant.10.clone.xb) | copy-start | bytes 442372

commit v2 on v1

--- a/solution.py
+++ b/solution.py
@@ -157,9 +157,10 @@
     return wy, wx, xb, wi
 
 
-def gather_kernel(
-    field, driver, east, north, wy, wx, coef, halo, ytile,
-    part, recv, edge, ysend, wind,
+def spectral_kernel(
+    field_in, driver_in, east_in, north_in, wy_in, wx_in, xb_in, wi_in, coef_out, advected,
+    coef, out, packed, flat, stores, field, driver, east, north, wy, wx, xb, wi,
+    part, recv, edge, ysend, wind, halo, ytile, full, winds, large, loads,
     a2a_s, a2a_r, halo_s, halo_r, y_s, y_r, z_s, z_r, p2_s, p2_r, p3_s, p3_r, core_s, core_r,
 ):
     gx = lax.axis_index("gx")
@@ -170,6 +171,37 @@
     fields, strip, band = field.shape
     levels = east.shape[0]
     own = fields // count
+    ext = strip + 8
+    total = fields + 2 * levels
+    chunk = 4 * own
+    chunks = fields // chunk
+
+    def load(src, dst, index):
+        return pltpu.make_async_copy(src, dst, loads.at[index])
+
+    def piece(src, dst, c, index):
+        rows = pl.ds(c * chunk, chunk)
+        return load(src.at[rows], dst.at[rows], index)
+
+    y_table = load(wy_in.at[gy], wy, 0)
+    x_table = load(wx_in, wx, 1)
+    small = [
+        load(east_in, east, 2),
+        load(north_in, north, 3),
+        load(xb_in.at[gx], xb, 4),
+        load(wi_in.at[gy], wi, 5),
+    ]
+    pieces = [
+        (piece(field_in, field, c, 6 + c), piece(driver_in, driver, c, 6 + chunks + c))
+        for c in range(chunks)
+    ]
+    y_table.start()
+    for a, b in pieces:
+        a.start()
+        b.start()
+    x_table.start()
+    for copy in small:
+        copy.start()
 
     barrier = pltpu.get_barrier_semaphore()
 
@@ -182,9 +214,11 @@
 
     lax.fori_loop(1, count, greet, 0)
 
-    wh, wl = wy[gy, 0], wy[gy, 1]
-    chunk = 4 * own
-    for c in range(fields // chunk):
+    y_table.wait()
+    wh, wl = wy[0], wy[1]
+    for c in range(chunks):
+        pieces[c][0].wait()
+        pieces[c][1].wait()
         rows = pl.ds(c * chunk, chunk)
         departure = driver[rows] - field[rows]
         lhs = jnp.concatenate([departure[:, : strip // 2], departure[:, strip // 2 :]], axis=2)
@@ -206,6 +240,9 @@
     lax.fori_loop(1, count, send, 0)
     recv[me] = part[me]
 
+    for copy in small:
+        copy.wait()
+    x_table.wait()
     row = lax.broadcasted_iota(jnp.int32, (levels, strip, band), 1) + gx * strip
     wind[pl.ds(0, levels)] = jnp.where(row == gxn * strip - 1, 0.0, east[...])
     col = lax.broadcasted_iota(jnp.int32, (levels, strip, band), 2) + gy * band
@@ -321,22 +358,123 @@
 
     for k in range(1, 4):
         z_copy(k, z).start()
-    for k in range(4):
-        if k:
-            z_copy(k, zs[k]).wait_recv()
+    second_a(0, x).start()
+    second_b(0, y).start()
+
+    for f in range(fields):
+        full[0, pl.ds(f * ext, strip)] = field[f]
+    for f in range(2 * levels):
+        full[0, pl.ds((fields + f) * ext, strip)] = wind[f]
+    blank = jnp.zeros((total, band), jnp.float32)
+    ycopy.wait()
+    for dy in range(2):
+
+        @pl.when(gx < gxn - 1)
+        def _():
+            halo_copy(0, dy).wait_send()
+            halo_copy(1, dy).wait_recv()
+
+        @pl.when(gx > 0)
+        def _():
+            halo_copy(1, dy).wait_send()
+            halo_copy(0, dy).wait_recv()
+
+    for d in range(2):
+        for k in range(2):
+            full[d, pl.ds(strip + k, total, stride=ext), :] = halo[1, d, k]
+            full[d, pl.ds(strip + 6 + k, total, stride=ext), :] = halo[0, d, k]
+        for k in range(2, 6):
+            full[d, pl.ds(strip + k, total, stride=ext), :] = blank
+
+    for k in range(1, 4):
+        z_copy(k, zs[k]).wait_recv()
         second_a(k, x).start()
         second_b(k, y).start()
+
+    gap = jnp.zeros((band - 16, 8 * strip), jnp.float32)
+    for b in range(total // 8):
+        tile = ytile[b]
+        spread = jnp.concatenate(
+            [jnp.where(gy == 0, tile, 0.0), gap, jnp.where(gy == 1, tile, 0.0)], axis=0
+        )
+        turned = spread.T
+        for i in range(8):
+            full[1, pl.ds((b * 8 + i) * ext, strip)] = turned[i * strip : (i + 1) * strip]
+
     for k in range(4):
         second_a(k, 1 - x).wait_recv()
         second_b(k, 1 - y).wait_recv()
         third_a(k, y).start()
         third_b(k, x).start()
+
+    def extended(f):
+        rows = pl.ds(pl.multiple_of(f * ext, 8), ext)
+        return jnp.concatenate([full[0, rows], full[1, rows]], axis=1)
+
+    for lev in range(levels):
+        u, v = extended(fields + lev), extended(fields + levels + lev)
+        winds[lev, 0] = jnp.maximum(u, 0.0)
+        winds[lev, 1] = jnp.minimum(u, 0.0)
+        winds[lev, 2] = jnp.maximum(v, 0.0)
+        winds[lev, 3] = jnp.minimum(v, 0.0)
+
+    lane = lax.broadcasted_iota(jnp.int32, (ext, 2 * MY), 1)
+
+    def store(src, dst, slot, index):
+        rows = pl.ds(pl.multiple_of(slot * (fields // 4), 8), fields // 4)
+        return pltpu.make_async_copy(src.at[rows], dst.at[rows], stores.at[index, slot])
+
+    def compute(slot):
+        base = slot * (fields // 4)
+
+        def inverse(i, carry):
+            rows = coef.at[slot, i // 4, (i // 2) % 2, i % 2]
+            blocks = [rows[pl.ds(j * hm, hm)] for j in range(own)]
+            for j in range(own):
+                flat[pl.ds(pl.multiple_of((i * own + j) * hm, hm), hm)] = blocks[j]
+            joined = jnp.concatenate(blocks, axis=1)
+            high, low = split(joined)
+            mixed = dot(xb[...], jnp.concatenate([high, low, high], axis=0))
+            stack = []
+            for j in range(own):
+                one = mixed[:, j * 2 * MY : (j + 1) * 2 * MY]
+                stack.append(jnp.where(lane < MY, one[:ext], one[ext:]))
+            high, low = split(jnp.concatenate(stack, axis=0))
+            got = dot(high, wi[0]) + (dot(low, wi[0]) + dot(high, wi[1]))
+            large[pl.ds(i * own, own)] = got.reshape(own, ext, gyn * band)
+            return carry
+
+        lax.fori_loop(0, fields // own // 4, inverse, 0, unroll=4)
+        held = pl.ds(pl.multiple_of(base, 8), fields // 4)
+        for j in range(hm):
+            packed[held, pl.ds(j * 2 * MY, 2 * MY)] = flat[pl.ds(j, fields // 4, stride=hm), :]
+        store(packed, coef_out, slot, 1).start()
+
+        def tracer(i, carry):
+            f = base + i
+            lev = f % levels
+            up, un, vp, vn = winds[lev, 0], winds[lev, 1], winds[lev, 2], winds[lev, 3]
+            q = extended(f) + large[i]
+            for _ in range(2):
+                flux = up * q + un * pltpu.roll(q, ext - 1, 0)
+                cross = vp * q + vn * pltpu.roll(q, gyn * band - 1, 1)
+                q = q - (flux - pltpu.roll(flux, 1, 0))
+                q = q - (cross - pltpu.roll(cross, 1, 1))
+            out[f] = q[:strip, :band]
+            return carry
+
+        lax.fori_loop(0, fields // 4, tracer, 0, unroll=6)
+        store(out, advected, slot, 0).start()
+
     for k in range(4):
         third_a(k, 1 - y).wait_recv()
         third_b(k, 1 - x).wait_recv()
         core_copy(k, c).start()
-    for k in range(4):
-        core_copy(k, 1 - c).wait_recv()
+        if k:
+            core_copy(k - 1, 1 - c).wait_recv()
+            compute(zs[k - 1])
+    core_copy(3, 1 - c).wait_recv()
+    compute(zs[3])
 
     for k in range(1, 4):
         z_copy(k, z).wait_send()
@@ -352,106 +490,9 @@
         return carry
 
     lax.fori_loop(1, count, drain, 0)
-    ycopy.wait()
-    for dy in range(2):
-
-        @pl.when(gx < gxn - 1)
-        def _():
-            halo_copy(0, dy).wait_send()
-            halo_copy(1, dy).wait_recv()
-
-        @pl.when(gx > 0)
-        def _():
-            halo_copy(1, dy).wait_send()
-            halo_copy(0, dy).wait_recv()
-
-
-def advect_kernel(
-    field, east, north, coef, halo, ytile, xb, wi, out, coef_out, side, other, large
-):
-    gx = lax.axis_index("gx")
-    gy = lax.axis_index("gy")
-    gxn, gyn = lax.axis_size("gx"), lax.axis_size("gy")
-    fields, strip, band = field.shape
-    levels = east.shape[0]
-    tracers = fields // levels
-    ext = strip + 8
-    hm = MX // 2
-    total = fields + 2 * levels
-    for j in range(hm):
-        coef_out[:, pl.ds(j * 2 * MY, 2 * MY)] = coef[pl.ds(j, fields, stride=hm), :]
-    side[...] = jnp.zeros(side.shape, jnp.float32)
-    for d in range(2):
-        for k in range(2):
-            side[d, pl.ds(k, total, stride=8), :] = halo[1, d, k]
-            side[d, pl.ds(6 + k, total, stride=8), :] = halo[0, d, k]
-    gap = jnp.zeros((band - 16, 8 * strip), jnp.float32)
-    for b in range(total // 8):
-        tile = ytile[b]
-        spread = jnp.concatenate(
-            [jnp.where(gy == 0, tile, 0.0), gap, jnp.where(gy == 1, tile, 0.0)], axis=0
-        )
-        other[pl.ds(b * 8, 8)] = spread.T.reshape(8, strip, band)
-
-    table = xb[gx]
-    wh, wl = wi[gy, 0], wi[gy, 1]
-    lane = lax.broadcasted_iota(jnp.int32, (ext, 2 * MY), 1)
-    group = 4
-
-    def inverse(g, carry):
-        stack = []
-        for h in range(group // 2):
-            f = g * group + 2 * h
-            two = jnp.concatenate(
-                [
-                    coef[pl.ds(pl.multiple_of(f * hm, hm), hm), :],
-                    coef[pl.ds(pl.multiple_of(f * hm + hm, hm), hm), :],
-                ],
-                axis=1,
-            )
-            high, low = split(two)
-            mixed = dot(table, jnp.concatenate([high, low, high], axis=0))
-            for i in range(2):
-                one = mixed[:, i * 2 * MY : (i + 1) * 2 * MY]
-                stack.append(jnp.where(lane < MY, one[:ext], one[ext:]))
-        high, low = split(jnp.concatenate(stack, axis=0))
-        got = dot(high, wh) + (dot(low, wh) + dot(high, wl))
-        large[pl.ds(g * group, group)] = got.reshape(group, ext, gyn * band)
-        return carry
-
-    lax.fori_loop(0, fields // group, inverse, 0, unroll=2)
-
-    xpos = lax.broadcasted_iota(jnp.int32, (strip, band), 0) + gx * strip
-    ypos = lax.broadcasted_iota(jnp.int32, (strip, band), 1) + gy * band
-
-    def extend(own, f):
-        rows = pl.ds(pl.multiple_of(f * 8, 8), 8)
-        edge = jnp.concatenate([side[0, rows, :], side[1, rows, :]], axis=1)
-        return jnp.concatenate([jnp.concatenate([own, other[f]], axis=1), edge], axis=0)
-
-    def level(lev, carry):
-        east_own = jnp.where(xpos == gxn * strip - 1, 0.0, east[lev])
-        north_own = jnp.where(ypos == gyn * band - 1, 0.0, north[lev])
-        u = extend(east_own, fields + lev)
-        v = extend(north_own, fields + levels + lev)
-        up, un = jnp.maximum(u, 0.0), jnp.minimum(u, 0.0)
-        vp, vn = jnp.maximum(v, 0.0), jnp.minimum(v, 0.0)
-
-        def tracer(t, inner):
-            f = t * levels + lev
-            q = extend(field[f], f) + large[f]
-            for _ in range(2):
-                flux = up * q + un * pltpu.roll(q, ext - 1, 0)
-                cross = vp * q + vn * pltpu.roll(q, gyn * band - 1, 1)
-                q = q - (flux - pltpu.roll(flux, 1, 0))
-                q = q - (cross - pltpu.roll(cross, 1, 1))
-            out[f] = q[:strip, :band]
-            return inner
-
-        lax.fori_loop(0, tracers, tracer, 0, unroll=2)
-        return carry
-
-    lax.fori_loop(0, levels, level, 0)
+    for k in range(4):
+        store(out, advected, zs[k], 0).wait()
+        store(packed, coef_out, zs[k], 1).wait()
 
 
 def fused(field, driver, east, north):
@@ -464,50 +505,53 @@
     wy, wx, xb, wi = tables(gxn, gyn, strip, band)
     flat = field.reshape(fields, strip, band)
     dma = pltpu.SemaphoreType.DMA
-    vmem = pl.BlockSpec(memory_space=pltpu.VMEM)
     f32 = jnp.float32
-    coef, halo, ytile = pl.pallas_call(
-        gather_kernel,
+    bf16 = jnp.bfloat16
+    hbm = pl.BlockSpec(memory_space=pltpu.HBM)
+    coeffs, advected = pl.pallas_call(
+        spectral_kernel,
         out_shape=(
-            jax.ShapeDtypeStruct((4, 2, 2, 2, own * MX // 2, 2 * MY), f32),
-            jax.ShapeDtypeStruct((2, 2, 2, total, band), f32),
-            jax.ShapeDtypeStruct((total // 8, 8, 8 * strip), f32),
+            jax.ShapeDtypeStruct((fields, MX * MY), f32),
+            jax.ShapeDtypeStruct((fields, strip, band), f32),
         ),
-        in_specs=[vmem] * 6,
-        out_specs=(vmem, vmem, vmem),
+        in_specs=[hbm] * 8,
+        out_specs=(hbm, hbm),
         scratch_shapes=[
+            pltpu.VMEM((4, 2, 2, 2, own * MX // 2, 2 * MY), f32),
+            pltpu.VMEM((fields, strip, band), f32),
+            pltpu.VMEM((fields, MX * MY), f32),
+            pltpu.VMEM((fields // 4 * MX // 2, 2 * MY), f32),
+            dma((2, 4)),
+            pltpu.VMEM((fields, strip, band), f32),
+            pltpu.VMEM((fields, strip, band), f32),
+            pltpu.VMEM((levels, strip, band), f32),
+            pltpu.VMEM((levels, strip, band), f32),
+            pltpu.VMEM(wy.shape[1:], bf16),
+            pltpu.VMEM(wx.shape, bf16),
+            pltpu.VMEM(xb.shape[1:], bf16),
+            pltpu.VMEM(wi.shape[1:], bf16),
             pltpu.VMEM((count, own, strip // 2, 2 * MY), f32),
             pltpu.VMEM((count, own, strip // 2, 2 * MY), f32),
             pltpu.VMEM((2, 2, total, band), f32),
             pltpu.VMEM((total // 8, 8, 8 * strip), f32),
             pltpu.VMEM((2 * levels, strip, band), f32),
+            pltpu.VMEM((2, 2, 2, total, band), f32),
+            pltpu.VMEM((total // 8, 8, 8 * strip), f32),
+            pltpu.VMEM((gyn, total * (strip + 8), band), f32),
+            pltpu.VMEM((levels, 4, strip + 8, gyn * band), f32),
+            pltpu.VMEM((fields // 4, strip + 8, gyn * band), f32),
+            dma((6 + 2 * (fields // (4 * own)),)),
             dma((count,)), dma((count,)), dma((2, 2)), dma((2, 2)), dma, dma,
             dma((4,)), dma((4,)), dma((2, 4)), dma((2, 4)), dma((2, 4)), dma((2, 4)),
             dma((4,)), dma((4,)),
         ],
         compiler_params=pltpu.CompilerParams(
-            collective_id=0, has_side_effects=True, vmem_limit_bytes=40 << 20
+            collective_id=0, has_side_effects=True, vmem_limit_bytes=62 << 20
         ),
-        name="spectral_gather",
-    )(flat, driver.reshape(fields, strip, band), east, north, jnp.asarray(wy), jnp.asarray(wx))
-    advected, coeffs = pl.pallas_call(
-        advect_kernel,
-        out_shape=(
-            jax.ShapeDtypeStruct((fields, strip, band), f32),
-            jax.ShapeDtypeStruct((fields, MX * MY), f32),
-        ),
-        in_specs=[vmem] * 8,
-        out_specs=(vmem, vmem),
-        scratch_shapes=[
-            pltpu.VMEM((gyn, total * 8, band), f32),
-            pltpu.VMEM((total, strip, band), f32),
-            pltpu.VMEM((fields, strip + 8, gyn * band), f32),
-        ],
-        compiler_params=pltpu.CompilerParams(vmem_limit_bytes=40 << 20),
-        name="advect",
+        name="spectral",
     )(
-        flat, east, north, coef.reshape(fields * MX // 2, 2 * MY), halo, ytile,
-        jnp.asarray(xb), jnp.asarray(wi),
+        flat, driver.reshape(fields, strip, band), east, north,
+        jnp.asarray(wy), jnp.asarray(wx), jnp.asarray(xb), jnp.asarray(wi),
     )
     return (
         advected.reshape(tracers, levels, strip, band),

time: 61.6 us -> 45.8 us (0.74)
  Pallas kernels: 54.6 us -> 41.2 us
  local copies, waits for them, and re-layouts: 5.93 us -> 3.36 us
    pallas_call x2 -> x1, Pallas kernels: 54.6 us -> 41.2 us  [fused(): pl.pallas_call(spectral_kernel, out_shape=(jax.ShapeDtypeStruct((fields,...]
    unnamed x16 -> x4, local copies, waits for them, and re-layouts: 5.93 us -> 3.36 us
where the time goes in v2:
time: 45.8 us; the launch traced here: 45.2 us
  Pallas kernels  41.2 us (90%)
  local copies, waits for them, and re-layouts  3.36 us (7%)
  between operations  0.65 us (1%)
    pallas_call x1, Pallas kernels, fused(): pl.pallas_call(spectral_kernel, out_shape=(jax.ShapeDtypeStruct((fields,...  41.2 us
    unnamed x4, local copies, waits for them, and re-layouts  3.36 us

profile of v2, /device:TPU:0, one launch (start us, length us, event | category | flops | bytes accessed | tf_op | source)
XLA Modules:
  0.0 45.2 jit_solution(14551748600811186092)
XLA Ops:
  0.6 41.2 %spectral.1 = (f32[96,4096]{1,0:T(8,128)}, f32[96,16,128]{2,1,0:T(8,128)}) custom-call(f32[96,16,128]{2,1,0:T(8,128)} %bitcast.6, f32[96,16,128]{2,1,0:T(8,128)} %bitcast.7, f32[16,16,128]{2,1,0:T(8,128)} %east_in.1, f32[16,16,128]{2,1,0:T(8,128)} %north_in.1, bf16[2,2,256,128]{3,2,1,0:T(8,128)(2,1)} %constant.8.clone.wy_in, ...), custom_call_target="tpu_custom_call" | custom-call | tf_op jit(solution)/shard_map/spectral/pallas_call | solution.py:511
  41.9 0.0 copy-start
  41.9 2.2 %copy.12 = f32[6,16,16,128]{3,2,1,0:T(8,128)} copy(f32[6,16,16,128]{3,2,1,0:T(8,128)} %bitcast.5) | data formatting | bytes 1572864
  44.1 0.0 copy-done
  44.1 1.1 %copy.13 = f32[6,16,4096]{2,1,0:T(8,128)} copy(f32[6,16,4096]{2,1,0:T(8,128)S(1)} %bitcast.4) | data formatting | bytes 3145728
Async XLA Ops:
  41.9 2.2 %copy-start = (f32[96,4096]{1,0:T(8,128)S(1)}, f32[96,4096]{1,0:T(8,128)}, u32[]{:S(2)}) copy-start(f32[96,4096]{1,0:T(8,128)} %get-tuple-element.5) | copy-start | bytes 4718596

commit v3 on v2

--- a/solution.py
+++ b/solution.py
@@ -259,26 +259,24 @@
         return pltpu.make_async_remote_copy(
             src_ref=edge.at[side], dst_ref=halo.at[side, dy],
             send_sem=halo_s.at[side, dy], recv_sem=halo_r.at[side, dy],
-            device_id=(peer, (gy + dy) % gyn), device_id_type=MESH,
-        )
-
-    for dy in range(2):
-
-        @pl.when(gx < gxn - 1)
-        def _():
-            halo_copy(0, dy).start()
-
-        @pl.when(gx > 0)
-        def _():
-            halo_copy(1, dy).start()
-
-        @pl.when(gx == 0)
-        def _():
-            halo[0, dy] = jnp.zeros(halo.shape[2:], jnp.float32)
-
-        @pl.when(gx == gxn - 1)
-        def _():
-            halo[1, dy] = jnp.zeros(halo.shape[2:], jnp.float32)
+            device_id=(peer, gy), device_id_type=MESH,
+        )
+
+    @pl.when(gx < gxn - 1)
+    def _():
+        halo_copy(0, 0).start()
+
+    @pl.when(gx > 0)
+    def _():
+        halo_copy(1, 0).start()
+
+    @pl.when(gx == 0)
+    def _():
+        halo[0, 0] = jnp.zeros(halo.shape[2:], jnp.float32)
+
+    @pl.when(gx == gxn - 1)
+    def _():
+        halo[1, 0] = jnp.zeros(halo.shape[2:], jnp.float32)
 
     for b in range((fields + 2 * levels) // 8):
         if b * 8 < fields:
@@ -291,7 +289,6 @@
         src_ref=ysend, dst_ref=ytile, send_sem=y_s, recv_sem=y_r,
         device_id=(gx, 1 - gy), device_id_type=MESH,
     )
-    ycopy.start()
 
     def receive(rel, carry):
         exchange((me + rel) % count, (me + rel) % count).wait_recv()
@@ -361,62 +358,61 @@
     second_a(0, x).start()
     second_b(0, y).start()
 
+    @pl.when(gx < gxn - 1)
+    def _():
+        halo_copy(0, 0).wait_send()
+        halo_copy(1, 0).wait_recv()
+
+    @pl.when(gx > 0)
+    def _():
+        halo_copy(1, 0).wait_send()
+        halo_copy(0, 0).wait_recv()
+
+    blocks_y = total // 8
+    for h in range(2):
+        for k in range(2):
+            turned = halo[h, 0, k].T
+            ysend[blocks_y + 2 * h + k] = jnp.where(gy == 0, turned[band - 8 :], turned[:8])
+    ycopy.start()
+
     for f in range(fields):
         full[0, pl.ds(f * ext, strip)] = field[f]
     for f in range(2 * levels):
         full[0, pl.ds((fields + f) * ext, strip)] = wind[f]
     blank = jnp.zeros((total, band), jnp.float32)
-    ycopy.wait()
-    for dy in range(2):
-
-        @pl.when(gx < gxn - 1)
-        def _():
-            halo_copy(0, dy).wait_send()
-            halo_copy(1, dy).wait_recv()
-
-        @pl.when(gx > 0)
-        def _():
-            halo_copy(1, dy).wait_send()
-            halo_copy(0, dy).wait_recv()
-
+    for k in range(2):
+        full[0, pl.ds(strip + k, total, stride=ext), :] = halo[1, 0, k]
+        full[0, pl.ds(strip + 6 + k, total, stride=ext), :] = halo[0, 0, k]
     for d in range(2):
-        for k in range(2):
-            full[d, pl.ds(strip + k, total, stride=ext), :] = halo[1, d, k]
-            full[d, pl.ds(strip + 6 + k, total, stride=ext), :] = halo[0, d, k]
         for k in range(2, 6):
             full[d, pl.ds(strip + k, total, stride=ext), :] = blank
-
-    for k in range(1, 4):
-        z_copy(k, zs[k]).wait_recv()
-        second_a(k, x).start()
-        second_b(k, y).start()
-
     gap = jnp.zeros((band - 16, 8 * strip), jnp.float32)
-    for b in range(total // 8):
+
+    def turn(b):
         tile = ytile[b]
-        spread = jnp.concatenate(
+        return jnp.concatenate(
             [jnp.where(gy == 0, tile, 0.0), gap, jnp.where(gy == 1, tile, 0.0)], axis=0
-        )
-        turned = spread.T
-        for i in range(8):
-            full[1, pl.ds((b * 8 + i) * ext, strip)] = turned[i * strip : (i + 1) * strip]
-
-    for k in range(4):
-        second_a(k, 1 - x).wait_recv()
-        second_b(k, 1 - y).wait_recv()
-        third_a(k, y).start()
-        third_b(k, x).start()
+        ).T
+
+    def assemble():
+        ycopy.wait()
+        for b in range(blocks_y):
+            turned = turn(b)
+            for i in range(8):
+                full[1, pl.ds((b * 8 + i) * ext, strip)] = turned[i * strip : (i + 1) * strip]
+        for k in range(2):
+            full[1, pl.ds(strip + k, total, stride=ext), :] = turn(blocks_y + 2 + k)
+            full[1, pl.ds(strip + 6 + k, total, stride=ext), :] = turn(blocks_y + k)
+        for lev in range(levels):
+            u, v = extended(fields + lev), extended(fields + levels + lev)
+            winds[lev, 0] = jnp.maximum(u, 0.0)
+            winds[lev, 1] = jnp.minimum(u, 0.0)
+            winds[lev, 2] = jnp.maximum(v, 0.0)
+            winds[lev, 3] = jnp.minimum(v, 0.0)
 
     def extended(f):
         rows = pl.ds(pl.multiple_of(f * ext, 8), ext)
         return jnp.concatenate([full[0, rows], full[1, rows]], axis=1)
-
-    for lev in range(levels):
-        u, v = extended(fields + lev), extended(fields + levels + lev)
-        winds[lev, 0] = jnp.maximum(u, 0.0)
-        winds[lev, 1] = jnp.minimum(u, 0.0)
-        winds[lev, 2] = jnp.maximum(v, 0.0)
-        winds[lev, 3] = jnp.minimum(v, 0.0)
 
     lane = lax.broadcasted_iota(jnp.int32, (ext, 2 * MY), 1)
 
@@ -466,15 +462,28 @@
         lax.fori_loop(0, fields // 4, tracer, 0, unroll=6)
         store(out, advected, slot, 0).start()
 
-    for k in range(4):
-        third_a(k, 1 - y).wait_recv()
-        third_b(k, 1 - x).wait_recv()
-        core_copy(k, c).start()
-        if k:
-            core_copy(k - 1, 1 - c).wait_recv()
-            compute(zs[k - 1])
-    core_copy(3, 1 - c).wait_recv()
-    compute(zs[3])
+    for step in range(1, 7):
+        if step < 4:
+            z_copy(step, zs[step]).wait_recv()
+            second_a(step, x).start()
+            second_b(step, y).start()
+        k = step - 1
+        if k < 4:
+            second_a(k, 1 - x).wait_recv()
+            second_b(k, 1 - y).wait_recv()
+            third_a(k, y).start()
+            third_b(k, x).start()
+        k = step - 2
+        if 0 <= k < 4:
+            third_a(k, 1 - y).wait_recv()
+            third_b(k, 1 - x).wait_recv()
+            core_copy(k, c).start()
+        if step == 2:
+            assemble()
+        k = step - 3
+        if k >= 0:
+            core_copy(k, 1 - c).wait_recv()
+            compute(zs[k])
 
     for k in range(1, 4):
         z_copy(k, z).wait_send()
@@ -533,15 +542,15 @@
             pltpu.VMEM((count, own, strip // 2, 2 * MY), f32),
             pltpu.VMEM((count, own, strip // 2, 2 * MY), f32),
             pltpu.VMEM((2, 2, total, band), f32),
-            pltpu.VMEM((total // 8, 8, 8 * strip), f32),
+            pltpu.VMEM((total // 8 + 4, 8, 8 * strip), f32),
             pltpu.VMEM((2 * levels, strip, band), f32),
-            pltpu.VMEM((2, 2, 2, total, band), f32),
-            pltpu.VMEM((total // 8, 8, 8 * strip), f32),
+            pltpu.VMEM((2, 1, 2, total, band), f32),
+            pltpu.VMEM((total // 8 + 4, 8, 8 * strip), f32),
             pltpu.VMEM((gyn, total * (strip + 8), band), f32),
             pltpu.VMEM((levels, 4, strip + 8, gyn * band), f32),
             pltpu.VMEM((fields // 4, strip + 8, gyn * band), f32),
             dma((6 + 2 * (fields // (4 * own)),)),
-            dma((count,)), dma((count,)), dma((2, 2)), dma((2, 2)), dma, dma,
+            dma((count,)), dma((count,)), dma((2, 1)), dma((2, 1)), dma, dma,
             dma((4,)), dma((4,)), dma((2, 4)), dma((2, 4)), dma((2, 4)), dma((2, 4)),
             dma((4,)), dma((4,)),
         ],

time: 45.8 us -> 45.3 us (0.989)
  no operation moved by 1% of the time
where the time goes in v3:
time: 45.3 us; the launch traced here: 45.1 us
  Pallas kernels  41.1 us (91%)
  local copies, waits for them, and re-layouts  3.36 us (7%)
  between operations  0.65 us (1%)
    pallas_call x1, Pallas kernels, fused(): pl.pallas_call(spectral_kernel, out_shape=(jax.ShapeDtypeStruct((fields,...  41.1 us
    unnamed x4, local copies, waits for them, and re-layouts  3.36 us

profile of v3, /device:TPU:0, one launch (start us, length us, event | category | flops | bytes accessed | tf_op | source)
XLA Modules:
  0.0 45.1 jit_solution(18080297475557087343)
XLA Ops:
  0.6 41.1 %spectral.1 = (f32[96,4096]{1,0:T(8,128)}, f32[96,16,128]{2,1,0:T(8,128)}) custom-call(f32[96,16,128]{2,1,0:T(8,128)} %bitcast.6, f32[96,16,128]{2,1,0:T(8,128)} %bitcast.7, f32[16,16,128]{2,1,0:T(8,128)} %east_in.1, f32[16,16,128]{2,1,0:T(8,128)} %north_in.1, bf16[2,2,256,128]{3,2,1,0:T(8,128)(2,1)} %constant.8.clone.wy_in, ...), custom_call_target="tpu_custom_call" | custom-call | tf_op jit(solution)/shard_map/spectral/pallas_call | solution.py:520
  41.8 0.0 copy-start
  41.8 2.2 %copy.12 = f32[6,16,16,128]{3,2,1,0:T(8,128)} copy(f32[6,16,16,128]{3,2,1,0:T(8,128)} %bitcast.5) | data formatting | bytes 1572864
  44.0 0.0 copy-done
  44.0 1.1 %copy.13 = f32[6,16,4096]{2,1,0:T(8,128)} copy(f32[6,16,4096]{2,1,0:T(8,128)S(1)} %bitcast.4) | data formatting | bytes 3145728
Async XLA Ops:
  41.8 2.2 %copy-start = (f32[96,4096]{1,0:T(8,128)S(1)}, f32[96,4096]{1,0:T(8,128)}, u32[]{:S(2)}) copy-start(f32[96,4096]{1,0:T(8,128)} %get-tuple-element.5) | copy-start | bytes 4718596

commit v4 on v3

--- a/solution.py
+++ b/solution.py
@@ -440,7 +440,7 @@
             large[pl.ds(i * own, own)] = got.reshape(own, ext, gyn * band)
             return carry
 
-        lax.fori_loop(0, fields // own // 4, inverse, 0, unroll=4)
+        lax.fori_loop(0, fields // own // 4, inverse, 0, unroll=8)
         held = pl.ds(pl.multiple_of(base, 8), fields // 4)
         for j in range(hm):
             packed[held, pl.ds(j * 2 * MY, 2 * MY)] = flat[pl.ds(j, fields // 4, stride=hm), :]
@@ -459,7 +459,7 @@
             out[f] = q[:strip, :band]
             return carry
 
-        lax.fori_loop(0, fields // 4, tracer, 0, unroll=6)
+        lax.fori_loop(0, fields // 4, tracer, 0, unroll=12)
         store(out, advected, slot, 0).start()
 
     for step in range(1, 7):
@@ -502,6 +502,24 @@
     for k in range(4):
         store(out, advected, zs[k], 0).wait()
         store(packed, coef_out, zs[k], 1).wait()
+
+
+def write_kernel(coef, advected, coef_out, advected_out, coef_v, advected_v, ins, outs):
+    inward, outward = [], []
+    arrays = ((coef, coef_v, coef_out), (advected, advected_v, advected_out))
+    for i, (src, mid, dst) in enumerate(arrays):
+        rows = src.shape[0] // 4
+        for k in range(4):
+            part = pl.ds(k * rows, rows)
+            inward.append(pltpu.make_async_copy(src.at[part], mid.at[part], ins.at[i, k]))
+            outward.append(pltpu.make_async_copy(mid.at[part], dst.at[part], outs.at[i, k]))
+    for copy in inward:
+        copy.start()
+    for a, b in zip(inward, outward):
+        a.wait()
+        b.start()
+    for copy in outward:
+        copy.wait()
 
 
 def fused(field, driver, east, north):
@@ -562,6 +580,23 @@
         flat, driver.reshape(fields, strip, band), east, north,
         jnp.asarray(wy), jnp.asarray(wx), jnp.asarray(xb), jnp.asarray(wi),
     )
+    coeffs, advected = pl.pallas_call(
+        write_kernel,
+        out_shape=(
+            jax.ShapeDtypeStruct((fields, MX * MY), f32),
+            jax.ShapeDtypeStruct((fields, strip, band), f32),
+        ),
+        in_specs=[hbm] * 2,
+        out_specs=(hbm, hbm),
+        scratch_shapes=[
+            pltpu.VMEM((fields, MX * MY), f32),
+            pltpu.VMEM((fields, strip, band), f32),
+            dma((2, 4)),
+            dma((2, 4)),
+        ],
+        compiler_params=pltpu.CompilerParams(vmem_limit_bytes=62 << 20),
+        name="write",
+    )(coeffs, advected)
     return (
         advected.reshape(tracers, levels, strip, band),
         coeffs.reshape(tracers, levels, MX * MY),

time: 45.3 us -> 42.8 us (0.945)
  local copies, waits for them, and re-layouts: 3.36 us -> 0 us
  Pallas kernels: 41.1 us -> 42 us
    unnamed x4 -> x0, local copies, waits for them, and re-layouts: 3.36 us -> none
    pallas_call x0 -> x1, Pallas kernels: none -> 2.52 us  [fused(): pl.pallas_call(write_kernel, out_shape=(jax.ShapeDtypeStruct((fields, MX...]
    pallas_call x1, Pallas kernels: 41.1 us -> 39.5 us  [fused(): pl.pallas_call(spectral_kernel, out_shape=(jax.ShapeDtypeStruct((fields,...]
where the time goes in v4:
time: 42.8 us; the launch traced here: 42.6 us
  Pallas kernels  42 us (98%)
  between operations  0.64 us (1%)
    pallas_call x1, Pallas kernels, fused(): pl.pallas_call(spectral_kernel, out_shape=(jax.ShapeDtypeStruct((fields,...  39.5 us
    pallas_call x1, Pallas kernels, fused(): pl.pallas_call(write_kernel, out_shape=(jax.ShapeDtypeStruct((fields, MX...  2.52 us

profile of v4, /device:TPU:0, one launch (start us, length us, event | category | flops | bytes accessed | tf_op | source)
XLA Modules:
  0.0 42.6 jit_solution(9378876208985548077)
XLA Ops:
  0.6 39.5 %spectral.1 = (f32[96,4096]{1,0:T(8,128)}, f32[96,16,128]{2,1,0:T(8,128)}) custom-call(f32[96,16,128]{2,1,0:T(8,128)} %bitcast.4, f32[96,16,128]{2,1,0:T(8,128)} %bitcast.5, f32[16,16,128]{2,1,0:T(8,128)} %east_in.1, f32[16,16,128]{2,1,0:T(8,128)} %north_in.1, bf16[2,2,256,128]{3,2,1,0:T(8,128)(2,1)} %constant.8.clone.wy_in, ...), custom_call_target="tpu_custom_call" | custom-call | tf_op jit(solution)/shard_map/spectral/pallas_call | solution.py:538
  40.1 2.5 %write.1 = (f32[96,4096]{1,0:T(8,128)}, f32[96,16,128]{2,1,0:T(8,128)}) custom-call(f32[96,4096]{1,0:T(8,128)} %get-tuple-element.6.coef, f32[96,16,128]{2,1,0:T(8,128)} %get-tuple-element.7.advected), custom_call_target="tpu_custom_call" | custom-call | tf_op jit(solution)/shard_map/write/pallas_call | solution.py:583
